TPU v7x, 32 devices: a whole 2x2x4 slice. The times are simulated.
32 devices in a mesh: tile: 8 (over y, x, core), plane: 4 (over z).
Axes of the slice: x: 2, y: 2, z: 4, core: 2. Of those that a mesh axis runs over, the one named last changes fastest.
Arguments:
- raw_tiles: bfloat16 [4, 64, 2, 16, 1024], P('plane', 'tile'), may hold values from 0.5 to 2.5
- flat_profile: bfloat16 [2, 16, 1024], P(None, 'plane'), may hold values from 0.5 to 1.5
- dark_profile: bfloat16 [2, 16, 1024], P(None, 'plane'), may hold values from 0 to 0.5
- destinations: int32 [4, 64, 1], P('plane', 'tile'), may hold values from 0 to 7, as said below
- positions: int32 [4, 64], P('plane', 'tile'), may hold values from 0 to 31
- levels: int32 [4, 64], P('plane', 'tile'), may hold values from 1 to 4
Outputs:
- stitched: bfloat16 [4, 2, 4096, 1024], P('plane', None, 'tile')
Inputs may be any that keep to these rules, and one draw needn't show every extreme that they name: `destinations`: the owner of a tile acquired by the device at index i of tile (aligned blocks of 8 tiles of a plane) is one of i - 2, ..., i + 2 or i + 4, modulo 8; among one device's tiles no owner is named more than 2 times, some owner exactly 2 times, and the owner i + 4 exactly 2 times.
All inputs are finite; a program needn't handle non-finite values.
Results may differ from a plain program's by a relative error of at most 0.0045.
Values may be sent and summed in bfloat16 or wider, within the bound.
No kernel may reach another device: no remote copies, remote signals or barrier semaphores. Data moves between devices by JAX's collectives and lax.ppermute only.
A program may use at most 64 MiB of HBM per device.

v0:
```python
import jax
import jax.numpy as jnp
from jax import lax
from jax.sharding import PartitionSpec as P

CR = 512
screen_weight = 0.5


def padded(cells, sides, width):
    for axis, dim in sides:
        count = lax.axis_size(axis)
        ends = count - 1
        head = lax.slice_in_dim(cells, 0, width, axis=dim)
        tail = lax.slice_in_dim(cells, cells.shape[dim] - width, cells.shape[dim], axis=dim)
        cells = jnp.concatenate(
            [
                lax.ppermute(tail, axis, [(i, (i + 1) % count) for i in range(ends)]),
                cells,
                lax.ppermute(head, axis, [((i + 1) % count, i) for i in range(ends)]),
            ],
            axis=dim,
        )
    return cells


def ramp_weights(tile_rows):
    tile_row = jnp.arange(tile_rows)
    return jnp.minimum(tile_row + 1, tile_rows - tile_row).astype(jnp.float32)


def apply_weights(camera, flat_full, dark_full, gains):
    corrected = (
        camera.astype(jnp.float32) - dark_full.astype(jnp.float32)[None]
    ) / flat_full.astype(jnp.float32)[None]
    scale = gains[:, None, None, None] * ramp_weights(camera.shape[2])[None, None, :, None]
    return (corrected * scale).astype(jnp.bfloat16)


def neighbour_sum(above, below, middle):
    zero_col = jnp.zeros(middle.shape[:2] + (1,), jnp.float32)
    shifted_left = jnp.concatenate([zero_col, middle[:, :, :-1]], 2)
    shifted_right = jnp.concatenate([middle[:, :, 1:], zero_col], 2)
    return above + below + shifted_left + shifted_right


def per_device(raw_tiles, flat_profile, dark_profile, destinations, positions, levels):
    camera = raw_tiles[0]
    owners = destinations[0, :, 0]
    grid_pos = positions[0]
    gains_int = levels[0]
    tile_count = camera.shape[0]
    tile_rows = camera.shape[2]
    owner_count = lax.axis_size("tile")
    capacity = max(2, tile_count // 4)
    canvas_rows = CR
    my_index = lax.axis_index("tile")
    flat_full, dark_full = (
        lax.all_gather(flat_profile, "plane", axis=1, tiled=True),
        lax.all_gather(dark_profile, "plane", axis=1, tiled=True),
    )
    same_dest = owners[:, None] == owners[None, :]
    earlier = jnp.arange(tile_count)[None, :] < jnp.arange(tile_count)[:, None]
    slot_rank = jnp.sum((same_dest & earlier).astype(jnp.int32), axis=1)
    slot_of = owners * capacity + slot_rank
    slot_total = owner_count * capacity
    matches = (slot_of[None, :] == jnp.arange(slot_total)[:, None]).astype(jnp.int32)
    slot_tile = jnp.sum(matches * jnp.arange(tile_count)[None, :], axis=1)
    occupied = jnp.sum(matches, axis=1)
    slot_gain = jnp.sum(matches * gains_int[None, :], axis=1)
    slot_pos = jnp.sum(matches * grid_pos[None, :], axis=1)
    slot_info = jnp.stack([slot_gain, slot_pos], 1).astype(jnp.bfloat16)
    occupied_mask = occupied.astype(jnp.bfloat16)[:, None, None, None]
    outgoing = jnp.take(camera, slot_tile, axis=0) * occupied_mask
    arrived, arrived_info = (
        lax.all_to_all(outgoing, "tile", split_axis=0, concat_axis=0, tiled=True),
        lax.all_to_all(slot_info, "tile", split_axis=0, concat_axis=0, tiled=True),
    )
    arrived_gain = arrived_info[:, 0].astype(jnp.float32)
    weighted = apply_weights(arrived, flat_full, dark_full, arrived_gain)
    first_rows = arrived_info[:, 1].astype(jnp.int32) * 16
    row_ids = jnp.arange(canvas_rows)[:, None, None]
    covered = row_ids == first_rows[None, :, None] + jnp.arange(tile_rows)[None, None, :]
    placement = covered.astype(jnp.bfloat16)
    accumulated = jnp.einsum(
        "ysr,scrx->cyx", placement, weighted, preferred_element_type=jnp.float32
    )
    row_gain = arrived_gain[:, None] * ramp_weights(tile_rows)[None, :]
    weight_sum = jnp.einsum("ysr,sr->y", covered.astype(jnp.float32), row_gain)
    blended = accumulated / jnp.maximum(weight_sum, 1.0)[None, :, None]
    extended = padded(blended.astype(jnp.bfloat16), (("tile", 1),), 3).astype(blended.dtype)
    global_rows = my_index * canvas_rows - 3 + jnp.arange(canvas_rows + 6)
    inside = ((global_rows >= 0) & (global_rows < owner_count * canvas_rows)).astype(jnp.float32)
    field = extended
    for sweep_id in range(3):
        kept = field.shape[1] - 2
        middle = field[:, 1:-1]
        neighbours = neighbour_sum(field[:, :-2], field[:, 2:], middle)
        source = extended[:, sweep_id + 1 : sweep_id + 1 + kept]
        mask_rows = inside[sweep_id + 1 : sweep_id + 1 + kept][None, :, None]
        field = (screen_weight * source + neighbours) / (screen_weight + 4.0) * mask_rows
    return field.astype(jnp.bfloat16)[None]


def solution(mesh):
    placed = (
        P("plane", "tile", None, None, None),
        P(None, "plane", None),
        P(None, "plane", None),
        P("plane", "tile", None),
        P("plane", "tile"),
        P("plane", "tile"),
    )
    return jax.shard_map(
        per_device,
        mesh=mesh,
        in_specs=placed,
        out_specs=P("plane", None, "tile", None),
        check_vma=False,
    )
```

profile of v0, /device:TPU:3, one launch (start us, length us, event | category | flops | bytes accessed | tf_op | source)
XLA Modules:
  0.0 81.8 jit_solution(9118618087000041648)
XLA Ops:
  0.0 0.9 %convert_reduce_fusion.1 = s32[8]{0:T(128)S(1)} fusion(s32[8]{0:T(128)} %bitcast.41), kind=kLoop, calls=%fused_computation.51 | loop fusion | flops 312 | bytes 64 | tf_op jit(solution)/shard_map/reduce_sum | solution.py:64
  0.9 0.7 multiply_add_fusion
  1.6 0.8 convert_reduce_fusion
  2.5 0.6 copy.27
  3.1 4.5 %all-to-all-start.1 = ((bf16[8,2,2]{1,2,0:T(2,128)(2,1)}), bf16[8,2,2]{1,2,0:T(2,128)(2,1)S(1)}, u32[]{:S(2)}, u32[]{:S(2)}) async-start(bf16[8,2,2]{1,2,0:T(2,128)(2,1)} %copy.27), calls=%async_computation.1 | async-start | bytes 8192 | tf_op jit(solution)/shard_map/all_to_all | solution.py:77
  7.9 0.7 copy.25
  8.6 0.7 copy.23
  9.4 10.6 %all_gather.6 = bf16[2,16,1024]{2,0,1:T(2,128)(2,1)S(1)} all-gather(bf16[2,4,1024]{2,0,1:T(2,128)(2,1)S(1)} %copy.23), channel_id=1, replica_groups=mesh['tile'=8,'plane'=4] {'plane'}, dimensions={1}, use_global_device_ids=true | all-gather | bytes 81920 | tf_op jit(solution)/shard_map/all_gather | solution.py:60
  20.0 10.2 %all_gather.7 = bf16[2,16,1024]{2,0,1:T(2,128)(2,1)S(1)} all-gather(bf16[2,4,1024]{2,0,1:T(2,128)(2,1)S(1)} %copy.25), channel_id=1, replica_groups=mesh['tile'=8,'plane'=4] {'plane'}, dimensions={1}, use_global_device_ids=true | all-gather | bytes 81920 | tf_op jit(solution)/shard_map/all_gather | solution.py:59
  30.2 0.6 gather_fusion
  30.9 1.2 %select_multiply_fusion = bf16[16,2,16,1024]{3,2,1,0:T(8,128)(2,1)} fusion(bf16[16,2,16,1024]{3,2,1,0:T(8,128)(2,1)S(1)} %gather_fusion, pred[16]{0:T(512)(128)(4,1)S(1)} %compare_and_fusion, bf16[16]{0:T(256)(128)(2,1)S(1)} %convert_element_type.77), kind=kLoop, calls=%fused_computation.29 | loop fusion | flops 1048576 | bytes 2097200 | tf_op jit(solution)/shard_map/mul | solution.py:74
  32.0 10.0 %all-to-all-start = ((bf16[16,2,16,1024]{3,2,1,0:T(8,128)(2,1)}), bf16[16,2,16,1024]{3,2,1,0:T(8,128)(2,1)S(1)}, u32[]{:S(2)}, u32[]{:S(2)}) async-start(bf16[16,2,16,1024]{3,2,1,0:T(8,128)(2,1)} %select_multiply_fusion), calls=%async_computation | async-start | bytes 2097152 | tf_op jit(solution)/shard_map/all_to_all | solution.py:76
  42.5 13.3 %all-to-all-done = bf16[16,2,16,1024]{3,2,1,0:T(8,128)(2,1)S(1)} async-done(((bf16[16,2,16,1024]{3,2,1,0:T(8,128)(2,1)}), bf16[16,2,16,1024]{3,2,1,0:T(8,128)(2,1)S(1)}, u32[]{:S(2)}, u32[]{:S(2)}) %all-to-all-start) | async-done | bytes 1048608 | tf_op jit(solution)/shard_map/all_to_all | solution.py:76
  55.8 0.9 %fusion.15 = bf16[2,512,1024]{2,1,0:T(8,128)(2,1)S(1)} fusion(f32[512]{0:T(512)S(1)} %broadcast_maximum_fusion, bf16[16,2,16,1024]{3,2,1,0:T(8,128)(2,1)S(1)} %all-to-all-done, f32[16,16]{1,0:T(8,128)S(1)} %broadcast_multiply_fusion, f32[2,16,1024]{2,1,0:T(8,128)S(1)} %copy_convert_fusion, f32[2,16,1024]{2,1,0:T(8,128)S(1)} %copy_convert_fusion.1, ...), kind=kOutput, calls=%fused_computation.25 | convolution fusion | flops 541720576 | bytes 3411968 | tf_op jit(solution)/shard_map/ysr,scrx->cyx/dot_general | solution.py:85
  56.8 3.5 %collective-permute-start = (bf16[2,3,1024]{2,1,0:T(4,128)(2,1)S(1)}, bf16[2,3,1024]{2,1,0:T(4,128)(2,1)S(1)}, u32[]{:S(2)}, u32[]{:S(2)}) collective-permute-start(bf16[2,3,1024]{2,1,0:T(4,128)(2,1)S(1)} %get-tuple-element.15), channel_id=1, source_target_pairs={{0,4},{4,8},{8,12},{12,16},{16,20},{20,24},{24,28},{1,5},{5,9},{9,... | collective-permute-start | bytes 36872 | tf_op jit(solution)/shard_map/ppermute | solution.py:18
  60.2 1.9 %collective-permute-start.1 = (bf16[2,3,1024]{2,1,0:T(4,128)(2,1)S(1)}, bf16[2,3,1024]{2,1,0:T(4,128)(2,1)S(1)}, u32[]{:S(2)}, u32[]{:S(2)}) collective-permute-start(bf16[2,3,1024]{2,1,0:T(4,128)(2,1)S(1)} %get-tuple-element.16), channel_id=1, source_target_pairs={{4,0},{8,4},{12,8},{16,12},{20,16},{24,20},{28,24},{5,1},{9,5},{13... | collective-permute-start | bytes 36872 | tf_op jit(solution)/shard_map/ppermute | solution.py:20
  62.2 4.0 %collective-permute-done.1 = bf16[2,3,1024]{2,1,0:T(4,128)(2,1)S(1)} collective-permute-done((bf16[2,3,1024]{2,1,0:T(4,128)(2,1)S(1)}, bf16[2,3,1024]{2,1,0:T(4,128)(2,1)S(1)}, u32[]{:S(2)}, u32[]{:S(2)}) %collective-permute-start.1) | collective-permute-done | bytes 12320 | tf_op jit(solution)/shard_map/ppermute | solution.py:20
  66.2 0.6 maximum_convert_fusion
  66.8 2.2 %fusion.34 = (f32[2,516,1023]{2,1,0:T(8,128)S(1)}, f32[2,516,1023]{2,1,0:T(8,128)S(1)}) fusion(f32[2,518,1024]{2,1,0:T(8,128)S(1)} %maximum_convert_fusion), kind=kLoop, calls=%fused_computation.71 | loop fusion | bytes 16891776 | tf_op jit(solution)/shard_map/slice | solution.py:42
  69.0 2.5 %fusion.7 = f32[2,516,1024]{2,1,0:T(8,128)S(1)} fusion(f32[2,518,1024]{2,1,0:T(8,128)S(1)} %maximum_convert_fusion, f32[2,516,1023]{2,1,0:T(8,128)S(1)} %get-tuple-element.14, f32[2,516,1023]{2,1,0:T(8,128)S(1)} %get-tuple-element.13, f32[516]{0:T(1024)S(1)} %slice_multiply_fusion.4), kind=kLoop, calls=%fused_computation.10 | loop fusion | flops 6340608 | bytes 25356240 | tf_op jit(solution)/shard_map/mul | solution.py:101
  71.5 2.2 %fusion.33 = (f32[2,514,1023]{2,1,0:T(8,128)S(1)}, f32[2,514,1023]{2,1,0:T(8,128)S(1)}) fusion(f32[2,516,1024]{2,1,0:T(8,128)S(1)} %fusion.7), kind=kLoop, calls=%fused_computation.70 | loop fusion | bytes 16826304 | tf_op jit(solution)/shard_map/slice | solution.py:42
  73.6 2.6 %fusion.3 = f32[2,514,1024]{2,1,0:T(8,128)S(1)} fusion(f32[2,516,1024]{2,1,0:T(8,128)S(1)} %fusion.7, f32[2,518,1024]{2,1,0:T(8,128)S(1)} %maximum_convert_fusion, f32[2,514,1023]{2,1,0:T(8,128)S(1)} %get-tuple-element.12, f32[2,514,1023]{2,1,0:T(8,128)S(1)} %get-tuple-element.11, f32[514]{0:T(1024)S(1)} %slice_multiply_fusion.3), kind=kLoop, calls=%fused_computation.5 | loop fusion | flops 6316032 | bytes 25257960 | tf_op jit(solution)/shard_map/mul | solution.py:101
  76.3 2.1 %fusion.32 = (f32[2,512,1023]{2,1,0:T(8,128)S(1)}, f32[2,512,1023]{2,1,0:T(8,128)S(1)}) fusion(f32[2,514,1024]{2,1,0:T(8,128)S(1)} %fusion.3), kind=kLoop, calls=%fused_computation.69 | loop fusion | bytes 16760832 | tf_op jit(solution)/shard_map/slice | solution.py:42
  78.4 3.5 %fusion.14 = bf16[1,2,512,1024]{3,2,1,0:T(8,128)(2,1)} fusion(f32[512]{0:T(512)S(1)} %slice_multiply_fusion.5, f32[2,512,1023]{2,1,0:T(8,128)S(1)} %get-tuple-element.10, f32[2,512,1023]{2,1,0:T(8,128)S(1)} %get-tuple-element.9, f32[2,514,1024]{2,1,0:T(8,128)S(1)} %fusion.3, f32[2,518,1024]{2,1,0:T(8,128)S(1)} %maximum_convert_fusion), kind=kLoop, calls=%fused_computation.24 | loop fusion | flops 7340032 | bytes 23062528 | tf_op jit(solution)/shard_map/broadcast_in_dim | solution.py:102
  (29 shorter events, 1.0 us)
Async XLA Ops:
  0.0 30.2 %copy-start = (bf16[1,8,2,16,1024]{4,3,2,1,0:T(8,128)(2,1)S(1)}, bf16[1,8,2,16,1024]{4,3,2,1,0:T(8,128)(2,1)}, u32[]{:S(2)}) copy-start(bf16[1,8,2,16,1024]{4,3,2,1,0:T(8,128)(2,1)} %param.6) | copy-start | bytes 1572868
  3.1 28.9 %all-to-all-start.1 = ((bf16[8,2,2]{1,2,0:T(2,128)(2,1)}), bf16[8,2,2]{1,2,0:T(2,128)(2,1)S(1)}, u32[]{:S(2)}, u32[]{:S(2)}) async-start(bf16[8,2,2]{1,2,0:T(2,128)(2,1)} %copy.27), calls=%async_computation.1 | async-start | bytes 8192 | tf_op jit(solution)/shard_map/all_to_all | solution.py:77
  32.0 23.8 %all-to-all-start = ((bf16[16,2,16,1024]{3,2,1,0:T(8,128)(2,1)}), bf16[16,2,16,1024]{3,2,1,0:T(8,128)(2,1)S(1)}, u32[]{:S(2)}, u32[]{:S(2)}) async-start(bf16[16,2,16,1024]{3,2,1,0:T(8,128)(2,1)} %select_multiply_fusion), calls=%async_computation | async-start | bytes 2097152 | tf_op jit(solution)/shard_map/all_to_all | solution.py:76
  56.8 5.5 %collective-permute-start = (bf16[2,3,1024]{2,1,0:T(4,128)(2,1)S(1)}, bf16[2,3,1024]{2,1,0:T(4,128)(2,1)S(1)}, u32[]{:S(2)}, u32[]{:S(2)}) collective-permute-start(bf16[2,3,1024]{2,1,0:T(4,128)(2,1)S(1)} %get-tuple-element.15), channel_id=1, source_target_pairs={{0,4},{4,8},{8,12},{12,16},{16,20},{20,24},{24,28},{1,5},{5,9},{9,... | collective-permute-start | bytes 36872 | tf_op jit(solution)/shard_map/ppermute | solution.py:18
  60.2 6.0 %collective-permute-start.1 = (bf16[2,3,1024]{2,1,0:T(4,128)(2,1)S(1)}, bf16[2,3,1024]{2,1,0:T(4,128)(2,1)S(1)}, u32[]{:S(2)}, u32[]{:S(2)}) collective-permute-start(bf16[2,3,1024]{2,1,0:T(4,128)(2,1)S(1)} %get-tuple-element.16), channel_id=1, source_target_pairs={{4,0},{8,4},{12,8},{16,12},{20,16},{24,20},{28,24},{5,1},{9,5},{13... | collective-permute-start | bytes 36872 | tf_op jit(solution)/shard_map/ppermute | solution.py:20
where the time goes:
time: 82.3 us; the launch traced here: 81.8 us
  blocking collectives  20.8 us (25%)
  starting transfers between devices  19.9 us (24%)
  waiting for transfers between devices  17.2 us (21%)
  other arithmetic  13.1 us (16%)
  local copies, waits for them, and re-layouts  9.41 us (11%)
  matrix products  1.16 us (1%)
    all_to_all x1, waiting for transfers between devices, per_device(): lax.all_to_all(outgoing, 'tile', split_axis=0, concat_axis=0, tiled=True)  13.3 us
    all_gather x1, blocking collectives, per_device(): lax.all_gather(dark_profile, 'plane', axis=1, tiled=True)  10.6 us
    all_gather x1, blocking collectives, per_device(): lax.all_gather(flat_profile, 'plane', axis=1, tiled=True)  10.2 us
    all_to_all x1, starting transfers between devices, per_device(): lax.all_to_all(outgoing, 'tile', split_axis=0, concat_axis=0, tiled=True)  9.97 us
    slice x3, local copies, waits for them, and re-layouts, neighbour_sum(): shifted_left = jnp.concatenate([zero_col, middle[:, :, :-1]], 2)  6.44 us
    mul x5, other arithmetic, per_device(): (screen_weight * source + neighbours) / (screen_weight + 4.0) * mask_rows  5.32 us
    all_to_all x1, starting transfers between devices, per_device(): lax.all_to_all(slot_info, 'tile', split_axis=0, concat_axis=0, tiled=True)  4.53 us
    ppermute x1, waiting for transfers between devices, padded(): lax.ppermute(head, axis, [((i + 1) % count, i) for i in range(ends)])  3.95 us
  transfers between devices with their start and end apart: 4, of which 2 were waited for; matrix products, arithmetic and copies ran while one was open for 5% of the time, Pallas kernels for 0%

commit v1 on v0

--- a/solution.py
+++ b/solution.py
@@ -5,6 +5,30 @@
 
 CR = 512
 screen_weight = 0.5
+
+
+def in_blocks(x, dim, devices):
+    dims = x.shape
+    parts = x.reshape(*dims[:dim], devices, dims[dim] // devices, *dims[dim + 1 :])
+    return jnp.moveaxis(parts, dim, 0)
+
+
+def joined_along(pieces, dim):
+    shape = list(pieces.shape[1:])
+    shape[dim] *= pieces.shape[0]
+    return jnp.moveaxis(pieces, 0, dim).reshape(shape)
+
+
+def rotated_exchange(array, axis, split_dim, concat_dim):
+    size, here = (lax.axis_size(axis), lax.axis_index(axis))
+    pieces = in_blocks(array, split_dim, size)
+    filled = pieces
+    for hop in range(1, size):
+        target, source = ((here + hop) % size, (here - hop) % size)
+        sent = lax.dynamic_index_in_dim(pieces, target, 0)
+        received = lax.ppermute(sent, axis, [(i, (i + hop) % size) for i in range(size)])
+        filled = lax.dynamic_update_slice_in_dim(filled, received, source, axis=0)
+    return joined_along(filled, concat_dim)
 
 
 def padded(cells, sides, width):
@@ -74,7 +98,7 @@
     outgoing = jnp.take(camera, slot_tile, axis=0) * occupied_mask
     arrived, arrived_info = (
         lax.all_to_all(outgoing, "tile", split_axis=0, concat_axis=0, tiled=True),
-        lax.all_to_all(slot_info, "tile", split_axis=0, concat_axis=0, tiled=True),
+        rotated_exchange(slot_info, "tile", 0, 0),
     )
     arrived_gain = arrived_info[:, 0].astype(jnp.float32)
     weighted = apply_weights(arrived, flat_full, dark_full, arrived_gain)

time: 82.3 us -> 76 us (0.923)
  waiting for transfers between devices: 17.2 us -> 6.51 us
  starting transfers between devices: 19.9 us -> 24.7 us
    ppermute x0 -> x7, starting transfers between devices: none -> 13.9 us  [rotated_exchange(): lax.ppermute(sent, axis, [(i, (i + hop) % size) for i in range(size)])]
    all_to_all x1, waiting for transfers between devices: 13.3 us -> 0.01 us  [per_device(): lax.all_to_all(outgoing, 'tile', split_axis=0, concat_axis=0, tiled=True)]
    all_to_all x1, starting transfers between devices: 9.97 us -> 4.2 us  [per_device(): lax.all_to_all(outgoing, 'tile', split_axis=0, concat_axis=0, tiled=True)]
    all_to_all x1 -> x0, starting transfers between devices: 4.53 us -> none  [per_device(): lax.all_to_all(slot_info, 'tile', split_axis=0, concat_axis=0, tiled=True)]
    ppermute x0 -> x7, waiting for transfers between devices: none -> 2.73 us  [rotated_exchange(): lax.ppermute(sent, axis, [(i, (i + hop) % size) for i in range(size)])]
    unnamed x4 -> x8, local copies, waits for them, and re-layouts: 1.47 us -> 0.04 us
    dynamic_update_slice x0 -> x8, local copies, waits for them, and re-layouts: none -> 1.23 us  [rotated_exchange(): filled = lax.dynamic_update_slice_in_dim(filled, received, source, axis=0)]
    ppermute x1, starting transfers between devices: 3.47 us -> 4.55 us  [padded(): lax.ppermute(tail, axis, [(i, (i + 1) % count) for i in range(ends)])]
  transfers between devices with their start and end apart: 4 -> 10, of which waited for: 2 -> 3; matrix products, arithmetic and copies ran while one was open for 5% -> 5% of each run, Pallas kernels for 0% -> 0%
where the time goes in v1:
time: 76 us; the launch traced here: 75.8 us
  starting transfers between devices  24.7 us (32%)
  blocking collectives  20.8 us (27%)
  other arithmetic  13.4 us (18%)
  local copies, waits for them, and re-layouts  8.8 us (12%)
  waiting for transfers between devices  6.51 us (9%)
  matrix products  1.16 us (2%)
    ppermute x7, starting transfers between devices, rotated_exchange(): lax.ppermute(sent, axis, [(i, (i + hop) % size) for i in range(size)])  13.9 us
    all_gather x1, blocking collectives, per_device(): lax.all_gather(dark_profile, 'plane', axis=1, tiled=True)  10.6 us
    all_gather x1, blocking collectives, per_device(): lax.all_gather(flat_profile, 'plane', axis=1, tiled=True)  10.2 us
    slice x3, local copies, waits for them, and re-layouts, neighbour_sum(): shifted_left = jnp.concatenate([zero_col, middle[:, :, :-1]], 2)  6.44 us
    mul x5, other arithmetic, per_device(): (screen_weight * source + neighbours) / (screen_weight + 4.0) * mask_rows  5.31 us
    ppermute x1, starting transfers between devices, padded(): lax.ppermute(tail, axis, [(i, (i + 1) % count) for i in range(ends)])  4.55 us
    all_to_all x1, starting transfers between devices, per_device(): lax.all_to_all(outgoing, 'tile', split_axis=0, concat_axis=0, tiled=True)  4.2 us
    ppermute x1, waiting for transfers between devices, padded(): lax.ppermute(head, axis, [((i + 1) % count, i) for i in range(ends)])  3.77 us
  transfers between devices with their start and end apart: 10, of which 3 were waited for; matrix products, arithmetic and copies ran while one was open for 5% of the time, Pallas kernels for 0%

profile of v1, /device:TPU:3, one launch (start us, length us, event | category | flops | bytes accessed | tf_op | source)
XLA Modules:
  0.0 75.8 jit_solution(7785738213039110962)
XLA Ops:
  0.1 0.9 %convert_reduce_fusion.1 = s32[8]{0:T(128)S(1)} fusion(s32[8]{0:T(128)} %bitcast.41), kind=kLoop, calls=%fused_computation.50 | loop fusion | flops 312 | bytes 64 | tf_op jit(solution)/shard_map/reduce_sum | solution.py:88
  1.0 0.7 multiply_add_fusion
  1.6 0.8 convert_reduce_fusion
  3.0 2.3 %collective-permute-start.2 = (bf16[1,2,2]{0,2,1:T(2,128)(2,1)S(1)}, bf16[1,2,2]{0,2,1:T(2,128)(2,1)S(1)}, u32[]{:S(2)}, u32[]{:S(2)}) collective-permute-start(bf16[1,2,2]{0,2,1:T(2,128)(2,1)S(1)} %get-tuple-element.21), channel_id=1, source_target_pairs={{0,12},{4,16},{8,20},{12,24},{16,28},{20,0},{24,4},{28,8},{1,13},{... | collective-permute-start | bytes 32 | tf_op jit(solution)/shard_map/ppermute | solution.py:29
  5.4 2.0 %collective-permute-start.6 = (bf16[1,2,2]{0,2,1:T(2,128)(2,1)S(1)}, bf16[1,2,2]{0,2,1:T(2,128)(2,1)S(1)}, u32[]{:S(2)}, u32[]{:S(2)}) collective-permute-start(bf16[1,2,2]{0,2,1:T(2,128)(2,1)S(1)} %get-tuple-element.17), channel_id=1, source_target_pairs={{0,28},{4,0},{8,4},{12,8},{16,12},{20,16},{24,20},{28,24},{1,29},{... | collective-permute-start | bytes 32 | tf_op jit(solution)/shard_map/ppermute | solution.py:29
  7.4 0.7 collective-permute-start
  8.7 1.2 %select_multiply_fusion = bf16[16,2,16,1024]{3,2,1,0:T(8,128)(2,1)} fusion(bf16[16,2,16,1024]{3,2,1,0:T(8,128)(2,1)S(1)} %gather_fusion, pred[16]{0:T(512)(128)(4,1)S(1)} %compare_and_fusion, bf16[16]{0:T(256)(128)(2,1)S(1)} %convert_element_type.77), kind=kLoop, calls=%fused_computation.29 | loop fusion | flops 1048576 | bytes 2097200 | tf_op jit(solution)/shard_map/mul | solution.py:98
  9.9 4.2 %all-to-all-start = ((bf16[16,2,16,1024]{3,2,1,0:T(8,128)(2,1)}), bf16[16,2,16,1024]{3,2,1,0:T(8,128)(2,1)S(1)}, u32[]{:S(2)}, u32[]{:S(2)}) async-start(bf16[16,2,16,1024]{3,2,1,0:T(8,128)(2,1)} %select_multiply_fusion), calls=%async_computation | async-start | bytes 2097152 | tf_op jit(solution)/shard_map/all_to_all | solution.py:100
  14.4 10.6 %all_gather.6 = bf16[2,16,1024]{2,0,1:T(2,128)(2,1)S(1)} all-gather(bf16[2,4,1024]{2,0,1:T(2,128)(2,1)S(1)} %copy.23), channel_id=1, replica_groups=mesh['tile'=8,'plane'=4] {'plane'}, dimensions={1}, use_global_device_ids=true | all-gather | bytes 81920 | tf_op jit(solution)/shard_map/all_gather | solution.py:84
  25.0 10.2 %all_gather.7 = bf16[2,16,1024]{2,0,1:T(2,128)(2,1)S(1)} all-gather(bf16[2,4,1024]{2,0,1:T(2,128)(2,1)S(1)} %copy.25), channel_id=1, replica_groups=mesh['tile'=8,'plane'=4] {'plane'}, dimensions={1}, use_global_device_ids=true | all-gather | bytes 81920 | tf_op jit(solution)/shard_map/all_gather | solution.py:83
  35.3 1.2 %collective-permute-start.1 = (bf16[1,2,2]{0,2,1:T(2,128)(2,1)S(1)}, bf16[1,2,2]{0,2,1:T(2,128)(2,1)S(1)}, u32[]{:S(2)}, u32[]{:S(2)}) collective-permute-start(bf16[1,2,2]{0,2,1:T(2,128)(2,1)S(1)} %get-tuple-element.19), channel_id=1, source_target_pairs={{0,8},{4,12},{8,16},{12,20},{16,24},{20,28},{24,0},{28,4},{1,9},{5... | collective-permute-start | bytes 32 | tf_op jit(solution)/shard_map/ppermute | solution.py:29
  36.8 1.4 %collective-permute-done.1 = bf16[1,2,2]{0,2,1:T(2,128)(2,1)S(1)} collective-permute-done((bf16[1,2,2]{0,2,1:T(2,128)(2,1)S(1)}, bf16[1,2,2]{0,2,1:T(2,128)(2,1)S(1)}, u32[]{:S(2)}, u32[]{:S(2)}) %collective-permute-start.1) | collective-permute-done | bytes 40 | tf_op jit(solution)/shard_map/ppermute | solution.py:29
  38.1 7.5 %collective-permute-start.4 = (bf16[1,2,2]{0,2,1:T(2,128)(2,1)S(1)}, bf16[1,2,2]{0,2,1:T(2,128)(2,1)S(1)}, u32[]{:S(2)}, u32[]{:S(2)}) collective-permute-start(bf16[1,2,2]{0,2,1:T(2,128)(2,1)S(1)} %fusion.33), channel_id=1, source_target_pairs={{0,20},{4,24},{8,28},{12,0},{16,4},{20,8},{24,12},{28,16},{1,21},{... | collective-permute-start | bytes 32 | tf_op jit(solution)/shard_map/ppermute | solution.py:29
  46.1 1.4 %collective-permute-done.4 = bf16[1,2,2]{0,2,1:T(2,128)(2,1)S(1)} collective-permute-done((bf16[1,2,2]{0,2,1:T(2,128)(2,1)S(1)}, bf16[1,2,2]{0,2,1:T(2,128)(2,1)S(1)}, u32[]{:S(2)}, u32[]{:S(2)}) %collective-permute-start.4) | collective-permute-done | bytes 40 | tf_op jit(solution)/shard_map/ppermute | solution.py:29
  48.7 0.9 %fusion.15 = bf16[2,512,1024]{2,1,0:T(8,128)(2,1)S(1)} fusion(f32[512]{0:T(512)S(1)} %broadcast_maximum_fusion, bf16[16,2,16,1024]{3,2,1,0:T(8,128)(2,1)S(1)} %all-to-all-done, f32[16,16]{1,0:T(8,128)S(1)} %broadcast_multiply_fusion, f32[2,16,1024]{2,1,0:T(8,128)S(1)} %copy_convert_fusion, f32[2,16,1024]{2,1,0:T(8,128)S(1)} %copy_convert_fusion.1, ...), kind=kOutput, calls=%fused_computation.25 | convolution fusion | flops 541720576 | bytes 3411968 | tf_op jit(solution)/shard_map/ysr,scrx->cyx/dot_general | solution.py:109
  49.6 4.5 %collective-permute-start.7 = (bf16[2,3,1024]{2,1,0:T(4,128)(2,1)S(1)}, bf16[2,3,1024]{2,1,0:T(4,128)(2,1)S(1)}, u32[]{:S(2)}, u32[]{:S(2)}) collective-permute-start(bf16[2,3,1024]{2,1,0:T(4,128)(2,1)S(1)} %get-tuple-element.15), channel_id=1, source_target_pairs={{0,4},{4,8},{8,12},{12,16},{16,20},{20,24},{24,28},{1,5},{5,9},{9,... | collective-permute-start | bytes 36872 | tf_op jit(solution)/shard_map/ppermute | solution.py:42
  54.2 2.1 %collective-permute-start.8 = (bf16[2,3,1024]{2,1,0:T(4,128)(2,1)S(1)}, bf16[2,3,1024]{2,1,0:T(4,128)(2,1)S(1)}, u32[]{:S(2)}, u32[]{:S(2)}) collective-permute-start(bf16[2,3,1024]{2,1,0:T(4,128)(2,1)S(1)} %get-tuple-element.16), channel_id=1, source_target_pairs={{4,0},{8,4},{12,8},{16,12},{20,16},{24,20},{28,24},{5,1},{9,5},{13... | collective-permute-start | bytes 36872 | tf_op jit(solution)/shard_map/ppermute | solution.py:44
  56.4 3.8 %collective-permute-done.8 = bf16[2,3,1024]{2,1,0:T(4,128)(2,1)S(1)} collective-permute-done((bf16[2,3,1024]{2,1,0:T(4,128)(2,1)S(1)}, bf16[2,3,1024]{2,1,0:T(4,128)(2,1)S(1)}, u32[]{:S(2)}, u32[]{:S(2)}) %collective-permute-start.8) | collective-permute-done | bytes 12320 | tf_op jit(solution)/shard_map/ppermute | solution.py:44
  60.8 2.2 %fusion.41 = (f32[2,516,1023]{2,1,0:T(8,128)S(1)}, f32[2,516,1023]{2,1,0:T(8,128)S(1)}) fusion(f32[2,518,1024]{2,1,0:T(8,128)S(1)} %maximum_convert_fusion), kind=kLoop, calls=%fused_computation.92 | loop fusion | bytes 16891776 | tf_op jit(solution)/shard_map/slice | solution.py:66
  62.9 2.5 %fusion.7 = f32[2,516,1024]{2,1,0:T(8,128)S(1)} fusion(f32[2,518,1024]{2,1,0:T(8,128)S(1)} %maximum_convert_fusion, f32[2,516,1023]{2,1,0:T(8,128)S(1)} %get-tuple-element.14, f32[2,516,1023]{2,1,0:T(8,128)S(1)} %get-tuple-element.13, f32[516]{0:T(1024)S(1)} %slice_multiply_fusion.4), kind=kLoop, calls=%fused_computation.10 | loop fusion | flops 6340608 | bytes 25356240 | tf_op jit(solution)/shard_map/mul | solution.py:125
  65.4 2.2 %fusion.40 = (f32[2,514,1023]{2,1,0:T(8,128)S(1)}, f32[2,514,1023]{2,1,0:T(8,128)S(1)}) fusion(f32[2,516,1024]{2,1,0:T(8,128)S(1)} %fusion.7), kind=kLoop, calls=%fused_computation.91 | loop fusion | bytes 16826304 | tf_op jit(solution)/shard_map/slice | solution.py:66
  67.6 2.6 %fusion.3 = f32[2,514,1024]{2,1,0:T(8,128)S(1)} fusion(f32[2,516,1024]{2,1,0:T(8,128)S(1)} %fusion.7, f32[2,518,1024]{2,1,0:T(8,128)S(1)} %maximum_convert_fusion, f32[2,514,1023]{2,1,0:T(8,128)S(1)} %get-tuple-element.12, f32[2,514,1023]{2,1,0:T(8,128)S(1)} %get-tuple-element.11, f32[514]{0:T(1024)S(1)} %slice_multiply_fusion.3), kind=kLoop, calls=%fused_computation.5 | loop fusion | flops 6316032 | bytes 25257960 | tf_op jit(solution)/shard_map/mul | solution.py:125
  70.2 2.1 %fusion.39 = (f32[2,512,1023]{2,1,0:T(8,128)S(1)}, f32[2,512,1023]{2,1,0:T(8,128)S(1)}) fusion(f32[2,514,1024]{2,1,0:T(8,128)S(1)} %fusion.3), kind=kLoop, calls=%fused_computation.90 | loop fusion | bytes 16760832 | tf_op jit(solution)/shard_map/slice | solution.py:66
  72.3 3.5 %fusion.14 = bf16[1,2,512,1024]{3,2,1,0:T(8,128)(2,1)} fusion(f32[512]{0:T(512)S(1)} %slice_multiply_fusion.5, f32[2,512,1023]{2,1,0:T(8,128)S(1)} %get-tuple-element.10, f32[2,512,1023]{2,1,0:T(8,128)S(1)} %get-tuple-element.9, f32[2,514,1024]{2,1,0:T(8,128)S(1)} %fusion.3, f32[2,518,1024]{2,1,0:T(8,128)S(1)} %maximum_convert_fusion), kind=kLoop, calls=%fused_computation.24 | loop fusion | flops 7340032 | bytes 23062528 | tf_op jit(solution)/shard_map/broadcast_in_dim | solution.py:126
  (56 shorter events, 4.0 us)
Async XLA Ops:
  0.0 8.1 %copy-start = (bf16[1,8,2,16,1024]{4,3,2,1,0:T(8,128)(2,1)S(1)}, bf16[1,8,2,16,1024]{4,3,2,1,0:T(8,128)(2,1)}, u32[]{:S(2)}) copy-start(bf16[1,8,2,16,1024]{4,3,2,1,0:T(8,128)(2,1)} %param.6) | copy-start | bytes 1572868
  0.0 14.4 %copy-start.1 = (bf16[2,4,1024]{2,1,0:T(4,128)(2,1)S(1)}, bf16[2,4,1024]{2,1,0:T(4,128)(2,1)}, u32[]{:S(2)}) copy-start(bf16[2,4,1024]{2,1,0:T(4,128)(2,1)} %param.7) | copy-start | bytes 49156
  0.0 14.4 %copy-start.2 = (bf16[2,4,1024]{2,1,0:T(4,128)(2,1)S(1)}, bf16[2,4,1024]{2,1,0:T(4,128)(2,1)}, u32[]{:S(2)}) copy-start(bf16[2,4,1024]{2,1,0:T(4,128)(2,1)} %param.8) | copy-start | bytes 49156
  2.9 44.8 %collective-permute-start.5 = (bf16[1,2,2]{0,2,1:T(2,128)(2,1)S(1)}, bf16[1,2,2]{0,2,1:T(2,128)(2,1)S(1)}, u32[]{:S(2)}, u32[]{:S(2)}) collective-permute-start(bf16[1,2,2]{0,2,1:T(2,128)(2,1)S(1)} %get-tuple-element.20), channel_id=1, source_target_pairs={{0,24},{4,28},{8,0},{12,4},{16,8},{20,12},{24,16},{28,20},{1,25},{... | collective-permute-start | bytes 32 | tf_op jit(solution)/shard_map/ppermute | solution.py:29
  3.0 42.9 %collective-permute-start.2 = (bf16[1,2,2]{0,2,1:T(2,128)(2,1)S(1)}, bf16[1,2,2]{0,2,1:T(2,128)(2,1)S(1)}, u32[]{:S(2)}, u32[]{:S(2)}) collective-permute-start(bf16[1,2,2]{0,2,1:T(2,128)(2,1)S(1)} %get-tuple-element.21), channel_id=1, source_target_pairs={{0,12},{4,16},{8,20},{12,24},{16,28},{20,0},{24,4},{28,8},{1,13},{... | collective-permute-start | bytes 32 | tf_op jit(solution)/shard_map/ppermute | solution.py:29
  5.3 40.6 %collective-permute-start.3 = (bf16[1,2,2]{0,2,1:T(2,128)(2,1)S(1)}, bf16[1,2,2]{0,2,1:T(2,128)(2,1)S(1)}, u32[]{:S(2)}, u32[]{:S(2)}) collective-permute-start(bf16[1,2,2]{0,2,1:T(2,128)(2,1)S(1)} %get-tuple-element.22), channel_id=1, source_target_pairs={{0,16},{4,20},{8,24},{12,28},{16,0},{20,4},{24,8},{28,12},{1,17},{... | collective-permute-start | bytes 32 | tf_op jit(solution)/shard_map/ppermute | solution.py:29
  5.4 42.5 %collective-permute-start.6 = (bf16[1,2,2]{0,2,1:T(2,128)(2,1)S(1)}, bf16[1,2,2]{0,2,1:T(2,128)(2,1)S(1)}, u32[]{:S(2)}, u32[]{:S(2)}) collective-permute-start(bf16[1,2,2]{0,2,1:T(2,128)(2,1)S(1)} %get-tuple-element.17), channel_id=1, source_target_pairs={{0,28},{4,0},{8,4},{12,8},{16,12},{20,16},{24,20},{28,24},{1,29},{... | collective-permute-start | bytes 32 | tf_op jit(solution)/shard_map/ppermute | solution.py:29
  7.4 28.0 %collective-permute-start = (bf16[1,2,2]{0,2,1:T(2,128)(2,1)S(1)}, bf16[1,2,2]{0,2,1:T(2,128)(2,1)S(1)}, u32[]{:S(2)}, u32[]{:S(2)}) collective-permute-start(bf16[1,2,2]{0,2,1:T(2,128)(2,1)S(1)} %get-tuple-element.18), channel_id=1, source_target_pairs={{0,4},{4,8},{8,12},{12,16},{16,20},{20,24},{24,28},{28,0},{1,5},{5... | collective-permute-start | bytes 32 | tf_op jit(solution)/shard_map/ppermute | solution.py:29
  9.9 38.8 %all-to-all-start = ((bf16[16,2,16,1024]{3,2,1,0:T(8,128)(2,1)}), bf16[16,2,16,1024]{3,2,1,0:T(8,128)(2,1)S(1)}, u32[]{:S(2)}, u32[]{:S(2)}) async-start(bf16[16,2,16,1024]{3,2,1,0:T(8,128)(2,1)} %select_multiply_fusion), calls=%async_computation | async-start | bytes 2097152 | tf_op jit(solution)/shard_map/all_to_all | solution.py:100
  35.3 2.8 %collective-permute-start.1 = (bf16[1,2,2]{0,2,1:T(2,128)(2,1)S(1)}, bf16[1,2,2]{0,2,1:T(2,128)(2,1)S(1)}, u32[]{:S(2)}, u32[]{:S(2)}) collective-permute-start(bf16[1,2,2]{0,2,1:T(2,128)(2,1)S(1)} %get-tuple-element.19), channel_id=1, source_target_pairs={{0,8},{4,12},{8,16},{12,20},{16,24},{20,28},{24,0},{28,4},{1,9},{5... | collective-permute-start | bytes 32 | tf_op jit(solution)/shard_map/ppermute | solution.py:29
  38.1 9.3 %collective-permute-start.4 = (bf16[1,2,2]{0,2,1:T(2,128)(2,1)S(1)}, bf16[1,2,2]{0,2,1:T(2,128)(2,1)S(1)}, u32[]{:S(2)}, u32[]{:S(2)}) collective-permute-start(bf16[1,2,2]{0,2,1:T(2,128)(2,1)S(1)} %fusion.33), channel_id=1, source_target_pairs={{0,20},{4,24},{8,28},{12,0},{16,4},{20,8},{24,12},{28,16},{1,21},{... | collective-permute-start | bytes 32 | tf_op jit(solution)/shard_map/ppermute | solution.py:29
  49.6 6.7 %collective-permute-start.7 = (bf16[2,3,1024]{2,1,0:T(4,128)(2,1)S(1)}, bf16[2,3,1024]{2,1,0:T(4,128)(2,1)S(1)}, u32[]{:S(2)}, u32[]{:S(2)}) collective-permute-start(bf16[2,3,1024]{2,1,0:T(4,128)(2,1)S(1)} %get-tuple-element.15), channel_id=1, source_target_pairs={{0,4},{4,8},{8,12},{12,16},{16,20},{20,24},{24,28},{1,5},{5,9},{9,... | collective-permute-start | bytes 36872 | tf_op jit(solution)/shard_map/ppermute | solution.py:42
  54.2 6.0 %collective-permute-start.8 = (bf16[2,3,1024]{2,1,0:T(4,128)(2,1)S(1)}, bf16[2,3,1024]{2,1,0:T(4,128)(2,1)S(1)}, u32[]{:S(2)}, u32[]{:S(2)}) collective-permute-start(bf16[2,3,1024]{2,1,0:T(4,128)(2,1)S(1)} %get-tuple-element.16), channel_id=1, source_target_pairs={{4,0},{8,4},{12,8},{16,12},{20,16},{24,20},{28,24},{5,1},{9,5},{13... | collective-permute-start | bytes 36872 | tf_op jit(solution)/shard_map/ppermute | solution.py:44
